TPU v7x, 256 devices: a whole 4x4x8 slice. The times are simulated.
256 devices in a mesh: cuts: 4 (over z_lo), amp: 64 (over y, x, z_hi, core).
Axes of the slice: x: 4, y: 4, z: 8 (z_hi: 2, z_lo: 4; z = z_hi * 4 + z_lo), core: 2. Of those that a mesh axis runs over, the one named last changes fastest.
Arguments:
- stem_state: bfloat16 [8, 32, 64, 128, 256], P('cuts', None, 'amp'), may hold values from -6 to 6
- gates: bfloat16 [8, 4, 2, 128, 128], P('cuts'), may hold values from -0.375 to 0.375
Outputs:
- amplitudes: float32 [32, 64, 128, 256], P('cuts', 'amp')
All inputs are finite; a program needn't handle non-finite values.
Results may differ from a plain program's by a relative error of at most 0.0049.
Values may be sent and summed in bfloat16 or wider, within the bound.
No kernel may reach another device: no remote copies, remote signals or barrier semaphores. Data moves between devices by JAX's collectives and lax.ppermute only.
A program may use at most 64 MiB of HBM per device.

v0:
```python
import functools

import jax
import jax.numpy as jnp
from jax import lax
from jax.experimental import pallas as pl
from jax.experimental.pallas import tpu as pltpu
from jax.sharding import Mesh, PartitionSpec as P


SIZES = (2, 2)
PLANE = ("y", "x", "core")
COLUMN = ("cuts", "zh")
BF = jnp.bfloat16
F32 = jnp.float32
LIMIT = pltpu.CompilerParams(vmem_limit_bytes=16 << 20)


def dot(left, right):
    return jnp.dot(left, right, preferred_element_type=F32)


def dot_t(left, right):
    return lax.dot_general(left, right, (((1,), (1,)), ((), ())), preferred_element_type=F32)


def iota(shape, axis):
    return lax.broadcasted_iota(jnp.int32, shape, axis)


def select_matrix(hit):
    return jnp.where(hit, 1.0, 0.0).astype(BF)


def before(gates_ref, state_ref, out_ref, rows_ref, second_ref, fourth_ref):
    @pl.when(pl.program_id(0) == 0)
    def prepare():
        row, col = iota((256, 128), 0), iota((256, 128), 1)
        pick = select_matrix(((row >> 3) * 4 + (row & 3)) == col)
        row_h = (row >> 2) & 1
        for s in range(2):
            for part in range(2):
                spread = dot(pick, gates_ref[s, 0, part])
                for h2 in range(2):
                    begin = part * 256 + h2 * 128
                    rows_ref[s, :, begin : begin + 128] = jnp.where(row_h == h2, spread, 0.0).astype(BF)
            for layer, out in ((1, second_ref), (3, fourth_ref)):
                real, imag = gates_ref[s, layer, 0], gates_ref[s, layer, 1]
                out[s, :128, :128] = real
                out[s, :128, 128:] = -imag
                out[s, 128:, :128] = imag
                out[s, 128:, 128:] = real

    results = []
    for s in range(2):
        firsts = []
        for k in range(4):
            state = state_ref[s, k, 0].reshape(256, 256)
            first = dot(rows_ref[s, :, :256], state) + dot(rows_ref[s, :, 256:], times_i(state))
            firsts.append(first.astype(BF))
        second = dot_t(jnp.concatenate(firsts, axis=0), second_ref[s]).astype(BF)
        results.append(dot_t(second, fourth_ref[s]).reshape(4, 32, 8, 256))
    for k in range(4):
        out_ref[:, k] = jnp.concatenate([results[0][k], results[1][k]], axis=1).astype(BF)


def join(z_ref, gates_ref, joint_ref):
    zh = z_ref[0] >> 2
    row, col = iota((512, 128), 0), iota((512, 128), 1)
    d, q = (row >> 3) & 31, (row >> 2) & 1
    pick_out = select_matrix((((d >> 1) * 4 + (row >> 8) * 2 + (d & 1)) * 2 + q) == col)
    row, col = iota((128, 512), 0), iota((128, 512), 1)
    d, q = col >> 4, col & 1
    pick_in = select_matrix((((d >> 1) * 4 + zh * 2 + (d & 1)) * 2 + q) == row)
    row, col = iota((512, 512), 0), iota((512, 512), 1)
    same = (row & 3) == ((col >> 1) & 3)
    col_s = (col >> 3) & 1
    for part in range(2):
        wide = []
        for s in range(2):
            wide.append(dot(dot(pick_out, gates_ref[s, 2, part]).astype(BF), pick_in))
        mixed = jnp.where(col_s == 0, wide[0], wide[1])
        joint_ref[:, part * 512 : part * 512 + 512] = jnp.where(same, mixed, 0.0).astype(BF)


def times_i(values):
    return jnp.concatenate([-values[:, 128:], values[:, :128]], axis=1)


def after(way, z_ref, state_ref, joint_ref, *out_refs):
    z = z_ref[0]
    states = [state_ref[:, (z + way * step) & 3].reshape(512, 256) for step in range(4)]
    turned = [times_i(state) for state in states]
    total = dot(joint_ref[:, :512], jnp.concatenate(states, axis=1))
    total = total + dot(joint_ref[:, 512:], jnp.concatenate(turned, axis=1))
    total = total.astype(BF)
    first = (4, 2 * way & 7)
    rest = [place for place in range(8) if place not in first]

    def put(place, value):
        if place in first:
            out_refs[0][first.index(place)] = value
        else:
            out_refs[1 + rest.index(place)][...] = value

    for step in range(4):
        low, high = (total[half * 256 : half * 256 + 256, step * 256 : step * 256 + 256] for half in range(2))
        ahead = (((z + way * step) & 3) - z) & 7
        ahead = jnp.full((256, 256), ahead, jnp.int32)
        place = (way * step) & 3
        put(place, jnp.where(ahead < 4, low, high))
        put(place + 4, jnp.where(ahead < 4, high, low))


def place(state_ref, out_ref):
    row, col = iota((256, 256), 0), iota((256, 256), 1)
    d, j, q, h2 = (row >> 2) & 31, (row >> 1) & 1, row & 1, row >> 7
    order = select_matrix((d * 8 + q * 4 + h2 * 2 + j) == col)
    for part in range(2):
        state = state_ref[:, pl.program_id(0) * 2 + part].astype(F32).reshape(256, 256).astype(BF)
        out_ref[part] = dot(order, state).reshape(2, 128, 256)


def ring(step):
    def at(z):
        return (z % 4) * 2 + z // 4

    return [(at(z), at((z + step) % 8)) for z in range(8)]


def add(*values):
    total = values[0].astype(F32)
    for value in values[1:]:
        total = total + value.astype(F32)
    return total.astype(BF)


def reduce_column(arrays, way):
    pair = arrays[0]
    rest = [place for place in range(8) if place not in (4, 2 * way & 7)]
    blocks = {place: array for place, array in zip(rest, arrays[1:])}

    def own(ahead):
        return blocks[ahead * way & 7]

    def shift(value, step):
        return lax.ppermute(value, COLUMN, ring(step * way))

    pair, far = shift(pair, 1), shift(own(-3), -1)
    near, far = add(pair[0], own(3)), add(far, own(-2))
    near, far = shift(near, 2), shift(far, -1)
    near, far = add(near, pair[1], own(1)), add(far, own(-1))
    near, far = shift(near, 1), shift(far, -1)
    return add(near, far, own(0))


def shape_of(shape, kind=BF):
    return jax.ShapeDtypeStruct(shape, kind)


def whole(shape):
    return pl.BlockSpec(shape, lambda *at: (0,) * len(shape))


def per_device_steps(stem_state, gates):
    z = (lax.axis_index("zh") * 4 + lax.axis_index("cuts")).astype(jnp.int32).reshape(1)
    scalar = pl.BlockSpec(memory_space=pltpu.SMEM)
    local = pl.BlockSpec(memory_space=pltpu.VMEM)
    joint = pl.pallas_call(
        join,
        in_specs=[scalar, local],
        out_specs=local,
        out_shape=pltpu.VMEM((512, 1024), BF),
        compiler_params=LIMIT,
        name="join",
    )(z, gates)
    state = stem_state.reshape(2, 4, 4, 2, 128, 256)
    sums = []
    for chunk, pairs in enumerate(SIZES):
        begin = sum(SIZES[:chunk])
        sent = pl.pallas_call(
            before,
            grid=(pairs,),
            in_specs=[
                whole((2, 4, 2, 128, 128)),
                pl.BlockSpec((2, 4, 1, 2, 128, 256), lambda hp, begin=begin: (0, 0, begin + hp, 0, 0, 0)),
            ],
            out_specs=pl.BlockSpec((32, 4, 16, 256), lambda hp: (0, hp, 0, 0)),
            out_shape=shape_of((32, pairs * 4, 16, 256)),
            scratch_shapes=[
                pltpu.VMEM((2, 256, 512), BF),
                pltpu.VMEM((2, 256, 256), BF),
                pltpu.VMEM((2, 256, 256), BF),
            ],
            name="before",
        )(gates, state)
        got = lax.all_to_all(sent, PLANE, split_axis=0, concat_axis=0, tiled=True)
        if chunk == 0:
            got = pltpu.with_memory_space_constraint(got, pltpu.HBM)
        for pair in range(pairs):
            way = 1 - 2 * (pair & 1)
            blocks = pl.pallas_call(
                functools.partial(after, way),
                grid=(1,),
                in_specs=[scalar, pl.BlockSpec((32, 4, 16, 256), lambda i, pair=pair: (0, pair, 0, 0)), local],
                out_specs=[local] * 7,
                out_shape=[pltpu.VMEM((2, 256, 256), BF)] + [pltpu.VMEM((256, 256), BF)] * 6,
                compiler_params=LIMIT,
            )(z, got, joint)
            total = reduce_column(blocks, way)
            sums.append(total.reshape(1, 32, 8, 256))
    home = jnp.swapaxes(jnp.concatenate(sums, axis=0), 0, 1)
    home = lax.all_to_all(home, PLANE, split_axis=0, concat_axis=0, tiled=True)
    placed = pl.pallas_call(
        place,
        grid=(2,),
        in_specs=[local],
        out_specs=pl.BlockSpec((2, 2, 128, 256), lambda step: (step, 0, 0, 0)),
        out_shape=shape_of((4, 2, 128, 256), F32),
        compiler_params=LIMIT,
        name="place",
    )(home)
    return placed.reshape(8, 1, 128, 256)


def solution(mesh):
    fine = Mesh(mesh.devices.reshape(4, 4, 4, 2, 2), ("cuts", "y", "x", "zh", "core"))
    amp = ("y", "x", "zh", "core")
    return jax.shard_map(
        per_device_steps,
        mesh=fine,
        in_specs=(P("cuts", None, amp, None, None), P("cuts", None, None, None, None)),
        out_specs=P("cuts", amp, None, None),
        check_vma=False,
    )
```

profile of v0, /device:TPU:1, one launch (start us, length us, event | category | flops | bytes accessed | tf_op | source)
XLA Modules:
  0.0 151.4 jit_solution(17640867802666735367)
XLA Ops:
  0.0 5.4 %before.3 = bf16[32,8,16,256]{3,2,1,0:T(8,128)(2,1)} custom-call(bf16[2,4,2,128,128]{4,3,2,1,0:T(8,128)(2,1)} %gates_ref.5, bf16[2,4,4,2,128,256]{5,4,3,2,1,0:T(8,128)(2,1)} %bitcast.55), custom_call_target="tpu_custom_call" | custom-call | tf_op jit(solution)/shard_map/before/pallas_call | solution.py:181
  5.4 8.6 %all-to-all-start.1 = ((bf16[32,8,16,256]{3,2,1,0:T(8,128)(2,1)}), bf16[32,8,16,256]{3,2,1,0:T(8,128)(2,1)S(1)}, u32[]{:S(2)}, u32[]{:S(2)}) async-start(bf16[32,8,16,256]{3,2,1,0:T(8,128)(2,1)} %before.3), calls=%async_computation.1 | async-start | bytes 4194304 | tf_op jit(solution)/shard_map/all_to_all | solution.py:197
  14.0 5.5 %before.2 = bf16[32,8,16,256]{3,2,1,0:T(8,128)(2,1)} custom-call(bf16[2,4,2,128,128]{4,3,2,1,0:T(8,128)(2,1)} %gates_ref.5, bf16[2,4,4,2,128,256]{5,4,3,2,1,0:T(8,128)(2,1)} %bitcast.56), custom_call_target="tpu_custom_call" | custom-call | tf_op jit(solution)/shard_map/before/pallas_call | solution.py:181
  19.5 23.1 %all-to-all-done.1.state_ref = bf16[32,8,16,256]{3,2,1,0:T(8,128)(2,1)S(1)} async-done(((bf16[32,8,16,256]{3,2,1,0:T(8,128)(2,1)}), bf16[32,8,16,256]{3,2,1,0:T(8,128)(2,1)S(1)}, u32[]{:S(2)}, u32[]{:S(2)}) %all-to-all-start.1) | async-done | bytes 2097184 | tf_op jit(solution)/shard_map/all_to_all | solution.py:197
  42.6 6.1 %all-to-all-start = ((bf16[32,8,16,256]{3,2,1,0:T(8,128)(2,1)}), bf16[32,8,16,256]{3,2,1,0:T(8,128)(2,1)}, u32[]{:S(2)}, u32[]{:S(2)}) async-start(bf16[32,8,16,256]{3,2,1,0:T(8,128)(2,1)} %before.2), calls=%async_computation | async-start | bytes 4194304 | tf_op jit(solution)/shard_map/all_to_all | solution.py:197
  49.7 1.3 join.1.joint_ref
  51.0 2.1 %shard_map.31 = (bf16[2,256,256]{2,1,0:T(8,128)(2,1)}, bf16[256,256]{1,0:T(8,128)(2,1)S(1)}, bf16[256,256]{1,0:T(8,128)(2,1)S(1)}, bf16[256,256]{1,0:T(8,128)(2,...) custom-call(s32[1]{0:T(128)} %bitcast.z_ref, ...), custom_call_target="tpu_custom_call" | custom-call | tf_op jit(solution)/shard_map/pallas_call | solution.py:202
  55.1 1.6 %collective-permute-start.21 = (bf16[256,256]{1,0:T(8,128)(2,1)}, bf16[256,256]{1,0:T(8,128)(2,1)}, u32[]{:S(2)}, u32[]{:S(2)}) collective-permute-start(bf16[256,256]{1,0:T(8,128)(2,1)} %get-tuple-element.57), channel_id=1, source_target_pairs={{0,64},{64,128},{128,192},{192,2},{2,66},{66,130},{130,194},{194,0... | collective-permute-start | bytes 393224 | tf_op jit(solution)/shard_map/ppermute | solution.py:147
  56.7 2.1 %shard_map.30 = (bf16[2,256,256]{2,1,0:T(8,128)(2,1)}, bf16[256,256]{1,0:T(8,128)(2,1)S(1)}, bf16[256,256]{1,0:T(8,128)(2,1)S(1)}, bf16[256,256]{1,0:T(8,128)(2,...) custom-call(s32[1]{0:T(128)} %bitcast.z_ref, ...), custom_call_target="tpu_custom_call" | custom-call | tf_op jit(solution)/shard_map/pallas_call | solution.py:202
  61.5 3.9 %collective-permute-start.15 = (bf16[256,256]{1,0:T(8,128)(2,1)}, bf16[256,256]{1,0:T(8,128)(2,1)S(1)}, u32[]{:S(2)}, u32[]{:S(2)}) collective-permute-start(bf16[256,256]{1,0:T(8,128)(2,1)} %get-tuple-element.50), channel_id=1, source_target_pairs={{0,194},{64,0},{128,64},{192,128},{2,192},{66,2},{130,66},{194,130... | collective-permute-start | bytes 393224 | tf_op jit(solution)/shard_map/ppermute | solution.py:147
  65.4 1.5 collective-permute-start.18
  66.9 10.1 %all-to-all-done.state_ref = bf16[32,8,16,256]{3,2,1,0:T(8,128)(2,1)} async-done(((bf16[32,8,16,256]{3,2,1,0:T(8,128)(2,1)}), bf16[32,8,16,256]{3,2,1,0:T(8,128)(2,1)}, u32[]{:S(2)}, u32[]{:S(2)}) %all-to-all-start) | async-done | bytes 2097184 | tf_op jit(solution)/shard_map/all_to_all | solution.py:197
  77.0 2.5 %shard_map.29 = (bf16[2,256,256]{2,1,0:T(8,128)(2,1)S(1)}, bf16[256,256]{1,0:T(8,128)(2,1)S(1)}, bf16[256,256]{1,0:T(8,128)(2,1)S(1)}, bf16[256,256]{1,0:T(8,128...) custom-call(s32[1]{0:T(128)} %bitcast.z_ref, ...), custom_call_target="tpu_custom_call" | custom-call | tf_op jit(solution)/shard_map/pallas_call | solution.py:202
  79.6 1.9 %collective-permute-start.9 = (bf16[256,256]{1,0:T(8,128)(2,1)S(1)}, bf16[256,256]{1,0:T(8,128)(2,1)S(1)}, u32[]{:S(2)}, u32[]{:S(2)}) collective-permute-start(bf16[256,256]{1,0:T(8,128)(2,1)S(1)} %get-tuple-element.43), channel_id=1, source_target_pairs={{0,64},{64,128},{128,192},{192,2},{2,66},{66,130},{130,194},{194,0... | collective-permute-start | bytes 393224 | tf_op jit(solution)/shard_map/ppermute | solution.py:147
  81.5 2.5 %shard_map.28 = (bf16[2,256,256]{2,1,0:T(8,128)(2,1)S(1)}, bf16[256,256]{1,0:T(8,128)(2,1)S(1)}, bf16[256,256]{1,0:T(8,128)(2,1)S(1)}, bf16[256,256]{1,0:T(8,128...) custom-call(s32[1]{0:T(128)} %bitcast.z_ref, ...), custom_call_target="tpu_custom_call" | custom-call | tf_op jit(solution)/shard_map/pallas_call | solution.py:202
  84.0 4.0 %collective-permute-start.3 = (bf16[256,256]{1,0:T(8,128)(2,1)S(1)}, bf16[256,256]{1,0:T(8,128)(2,1)S(1)}, u32[]{:S(2)}, u32[]{:S(2)}) collective-permute-start(bf16[256,256]{1,0:T(8,128)(2,1)S(1)} %get-tuple-element.36), channel_id=1, source_target_pairs={{0,194},{64,0},{128,64},{192,128},{2,192},{66,2},{130,66},{194,130... | collective-permute-start | bytes 393224 | tf_op jit(solution)/shard_map/ppermute | solution.py:147
  89.0 1.5 %collective-permute-start.6 = (bf16[2,256,256]{2,1,0:T(8,128)(2,1)S(1)}, bf16[2,256,256]{2,1,0:T(8,128)(2,1)S(1)}, u32[]{:S(2)}, u32[]{:S(2)}) collective-permute-start(bf16[2,256,256]{2,1,0:T(8,128)(2,1)S(1)} %get-tuple-element.40), channel_id=1, source_target_pairs={{0,194},{64,0},{128,64},{192,128},{2,192},{66,2},{130,66},{194,130... | collective-permute-start | bytes 786440 | tf_op jit(solution)/shard_map/ppermute | solution.py:147
  90.9 2.7 %collective-permute-start.16 = (bf16[256,256]{1,0:T(8,128)(2,1)S(1)}, bf16[256,256]{1,0:T(8,128)(2,1)S(1)}, u32[]{:S(2)}, u32[]{:S(2)}) collective-permute-start(bf16[256,256]{1,0:T(8,128)(2,1)S(1)} %add_convert_fusion.5), channel_id=1, source_target_pairs={{0,194},{64,0},{128,64},{192,128},{2,192},{66,2},{130,66},{194,130... | collective-permute-start | bytes 393224 | tf_op jit(solution)/shard_map/ppermute | solution.py:147
  93.8 2.5 %collective-permute-done.6 = bf16[2,256,256]{2,1,0:T(8,128)(2,1)S(1)} collective-permute-done((bf16[2,256,256]{2,1,0:T(8,128)(2,1)S(1)}, bf16[2,256,256]{2,1,0:T(8,128)(2,1)S(1)}, u32[]{:S(2)}, u32[]{:S(2)}) %collective-permute-start.6) | collective-permute-done | bytes 262176 | tf_op jit(solution)/shard_map/ppermute | solution.py:147
  96.3 3.4 %collective-permute-start.4 = (bf16[256,256]{1,0:T(8,128)(2,1)S(1)}, bf16[256,256]{1,0:T(8,128)(2,1)S(1)}, u32[]{:S(2)}, u32[]{:S(2)}) collective-permute-start(bf16[256,256]{1,0:T(8,128)(2,1)S(1)} %add_convert_fusion.11), channel_id=1, source_target_pairs={{0,194},{64,0},{128,64},{192,128},{2,192},{66,2},{130,66},{194,130... | collective-permute-start | bytes 393224 | tf_op jit(solution)/shard_map/ppermute | solution.py:147
  99.9 2.4 %collective-permute-start.13 = (bf16[256,256]{1,0:T(8,128)(2,1)S(1)}, bf16[256,256]{1,0:T(8,128)(2,1)S(1)}, u32[]{:S(2)}, u32[]{:S(2)}) collective-permute-start(bf16[256,256]{1,0:T(8,128)(2,1)S(1)} %fusion.5), channel_id=1, source_target_pairs={{0,128},{64,192},{128,2},{192,66},{2,130},{66,194},{130,0},{194,64... | collective-permute-start | bytes 393224 | tf_op jit(solution)/shard_map/ppermute | solution.py:147
  102.4 1.3 collective-permute-start.7
  105.1 2.1 %collective-permute-done.19 = bf16[256,256]{1,0:T(8,128)(2,1)S(1)} collective-permute-done((bf16[256,256]{1,0:T(8,128)(2,1)S(1)}, bf16[256,256]{1,0:T(8,128)(2,1)S(1)}, u32[]{:S(2)}, u32[]{:S(2)}) %collective-permute-start.19) | collective-permute-done | bytes 131104 | tf_op jit(solution)/shard_map/ppermute | solution.py:147
  107.9 1.6 %collective-permute-start.11 = (bf16[256,256]{1,0:T(8,128)(2,1)S(1)}, bf16[256,256]{1,0:T(8,128)(2,1)S(1)}, u32[]{:S(2)}, u32[]{:S(2)}) collective-permute-start(bf16[256,256]{1,0:T(8,128)(2,1)S(1)} %add_convert_fusion.7), channel_id=1, source_target_pairs={{0,64},{64,128},{128,192},{192,2},{2,66},{66,130},{130,194},{194,0... | collective-permute-start | bytes 393224 | tf_op jit(solution)/shard_map/ppermute | solution.py:147
  109.5 2.7 %collective-permute-done.7 = bf16[256,256]{1,0:T(8,128)(2,1)S(1)} collective-permute-done((bf16[256,256]{1,0:T(8,128)(2,1)S(1)}, bf16[256,256]{1,0:T(8,128)(2,1)S(1)}, u32[]{:S(2)}, u32[]{:S(2)}) %collective-permute-start.7) | collective-permute-done | bytes 131104 | tf_op jit(solution)/shard_map/ppermute | solution.py:147
  113.4 3.6 %collective-permute-start.20 = (bf16[256,256]{1,0:T(8,128)(2,1)S(1)}, bf16[256,256]{1,0:T(8,128)(2,1)S(1)}, u32[]{:S(2)}, u32[]{:S(2)}) collective-permute-start(bf16[256,256]{1,0:T(8,128)(2,1)S(1)} %fusion.1), channel_id=1, source_target_pairs={{0,194},{64,0},{128,64},{192,128},{2,192},{66,2},{130,66},{194,130... | collective-permute-start | bytes 393224 | tf_op jit(solution)/shard_map/ppermute | solution.py:147
  117.8 2.7 %collective-permute-done.20 = bf16[256,256]{1,0:T(8,128)(2,1)S(1)} collective-permute-done((bf16[256,256]{1,0:T(8,128)(2,1)S(1)}, bf16[256,256]{1,0:T(8,128)(2,1)S(1)}, u32[]{:S(2)}, u32[]{:S(2)}) %collective-permute-start.20) | collective-permute-done | bytes 131104 | tf_op jit(solution)/shard_map/ppermute | solution.py:147
  120.5 3.1 %collective-permute-start.8 = (bf16[256,256]{1,0:T(8,128)(2,1)S(1)}, bf16[256,256]{1,0:T(8,128)(2,1)S(1)}, u32[]{:S(2)}, u32[]{:S(2)}) collective-permute-start(bf16[256,256]{1,0:T(8,128)(2,1)S(1)} %fusion.7), channel_id=1, source_target_pairs={{0,194},{64,0},{128,64},{192,128},{2,192},{66,2},{130,66},{194,130... | collective-permute-start | bytes 393224 | tf_op jit(solution)/shard_map/ppermute | solution.py:147
  123.9 2.2 %collective-permute-done.8 = bf16[256,256]{1,0:T(8,128)(2,1)S(1)} collective-permute-done((bf16[256,256]{1,0:T(8,128)(2,1)S(1)}, bf16[256,256]{1,0:T(8,128)(2,1)S(1)}, u32[]{:S(2)}, u32[]{:S(2)}) %collective-permute-start.8) | collective-permute-done | bytes 131104 | tf_op jit(solution)/shard_map/ppermute | solution.py:147
  126.1 3.5 %collective-permute-done.2 = bf16[256,256]{1,0:T(8,128)(2,1)S(1)} collective-permute-done((bf16[256,256]{1,0:T(8,128)(2,1)S(1)}, bf16[256,256]{1,0:T(8,128)(2,1)S(1)}, u32[]{:S(2)}, u32[]{:S(2)}) %collective-permute-start.2) | collective-permute-done | bytes 131104 | tf_op jit(solution)/shard_map/ppermute | solution.py:147
  129.7 20.5 %all_to_all.15.state_ref = bf16[32,4,8,256]{3,2,1,0:T(8,128)(2,1)S(1)} all-to-all(bf16[32,4,8,256]{3,2,1,0:T(8,128)(2,1)S(1)} %maximum_bitcast_fusion), channel_id=1, replica_groups=mesh['cuts'=4,'y'=4,'x'=4,'zh'=2,'core'=2] {'y','x','core'}, dimensions={0} | all-to-all | bytes 1048576 | tf_op jit(solution)/shard_map/all_to_all | solution.py:213
  150.2 1.3 place.1
  (80 shorter events, 11.8 us)
Async XLA Ops:
  5.4 37.2 %all-to-all-start.1 = ((bf16[32,8,16,256]{3,2,1,0:T(8,128)(2,1)}), bf16[32,8,16,256]{3,2,1,0:T(8,128)(2,1)S(1)}, u32[]{:S(2)}, u32[]{:S(2)}) async-start(bf16[32,8,16,256]{3,2,1,0:T(8,128)(2,1)} %before.3), calls=%async_computation.1 | async-start | bytes 4194304 | tf_op jit(solution)/shard_map/all_to_all | solution.py:197
  42.6 34.4 %all-to-all-start = ((bf16[32,8,16,256]{3,2,1,0:T(8,128)(2,1)}), bf16[32,8,16,256]{3,2,1,0:T(8,128)(2,1)}, u32[]{:S(2)}, u32[]{:S(2)}) async-start(bf16[32,8,16,256]{3,2,1,0:T(8,128)(2,1)} %before.2), calls=%async_computation | async-start | bytes 4194304 | tf_op jit(solution)/shard_map/all_to_all | solution.py:197
  55.1 28.9 %collective-permute-start.21 = (bf16[256,256]{1,0:T(8,128)(2,1)}, bf16[256,256]{1,0:T(8,128)(2,1)}, u32[]{:S(2)}, u32[]{:S(2)}) collective-permute-start(bf16[256,256]{1,0:T(8,128)(2,1)} %get-tuple-element.57), channel_id=1, source_target_pairs={{0,64},{64,128},{128,192},{192,2},{2,66},{66,130},{130,194},{194,0... | collective-permute-start | bytes 393224 | tf_op jit(solution)/shard_map/ppermute | solution.py:147
  61.5 27.5 %collective-permute-start.15 = (bf16[256,256]{1,0:T(8,128)(2,1)}, bf16[256,256]{1,0:T(8,128)(2,1)S(1)}, u32[]{:S(2)}, u32[]{:S(2)}) collective-permute-start(bf16[256,256]{1,0:T(8,128)(2,1)} %get-tuple-element.50), channel_id=1, source_target_pairs={{0,194},{64,0},{128,64},{192,128},{2,192},{66,2},{130,66},{194,130... | collective-permute-start | bytes 393224 | tf_op jit(solution)/shard_map/ppermute | solution.py:147
  65.4 25.4 %collective-permute-start.18 = (bf16[2,256,256]{2,1,0:T(8,128)(2,1)}, bf16[2,256,256]{2,1,0:T(8,128)(2,1)S(1)}, u32[]{:S(2)}, u32[]{:S(2)}) collective-permute-start(bf16[2,256,256]{2,1,0:T(8,128)(2,1)} %get-tuple-element.54), channel_id=1, source_target_pairs={{0,194},{64,0},{128,64},{192,128},{2,192},{66,2},{130,66},{194,130... | collective-permute-start | bytes 786440 | tf_op jit(solution)/shard_map/ppermute | solution.py:147
  66.9 26.7 %collective-permute-start.12 = (bf16[2,256,256]{2,1,0:T(8,128)(2,1)}, bf16[2,256,256]{2,1,0:T(8,128)(2,1)S(1)}, u32[]{:S(2)}, u32[]{:S(2)}) collective-permute-start(bf16[2,256,256]{2,1,0:T(8,128)(2,1)} %get-tuple-element.47), channel_id=1, source_target_pairs={{0,64},{64,128},{128,192},{192,2},{2,66},{66,130},{130,194},{194,0... | collective-permute-start | bytes 786440 | tf_op jit(solution)/shard_map/ppermute | solution.py:147
  79.6 11.0 %copy-start.6 = (bf16[256,256]{1,0:T(8,128)(2,1)S(1)}, bf16[256,256]{1,0:T(8,128)(2,1)}, u32[]{:S(2)}) copy-start(bf16[256,256]{1,0:T(8,128)(2,1)} %copy-done.5) | copy-start | bytes 393220
  79.6 14.2 %copy-start.2 = (bf16[256,256]{1,0:T(8,128)(2,1)S(1)}, bf16[256,256]{1,0:T(8,128)(2,1)}, u32[]{:S(2)}) copy-start(bf16[256,256]{1,0:T(8,128)(2,1)} %copy-done.1) | copy-start | bytes 393220
  79.6 11.0 %collective-permute-start.9 = (bf16[256,256]{1,0:T(8,128)(2,1)S(1)}, bf16[256,256]{1,0:T(8,128)(2,1)S(1)}, u32[]{:S(2)}, u32[]{:S(2)}) collective-permute-start(bf16[256,256]{1,0:T(8,128)(2,1)S(1)} %get-tuple-element.43), channel_id=1, source_target_pairs={{0,64},{64,128},{128,192},{192,2},{2,66},{66,130},{130,194},{194,0... | collective-permute-start | bytes 393224 | tf_op jit(solution)/shard_map/ppermute | solution.py:147
  84.0 6.7 %collective-permute-start.3 = (bf16[256,256]{1,0:T(8,128)(2,1)S(1)}, bf16[256,256]{1,0:T(8,128)(2,1)S(1)}, u32[]{:S(2)}, u32[]{:S(2)}) collective-permute-start(bf16[256,256]{1,0:T(8,128)(2,1)S(1)} %get-tuple-element.36), channel_id=1, source_target_pairs={{0,194},{64,0},{128,64},{192,128},{2,192},{66,2},{130,66},{194,130... | collective-permute-start | bytes 393224 | tf_op jit(solution)/shard_map/ppermute | solution.py:147
  89.0 7.3 %collective-permute-start.6 = (bf16[2,256,256]{2,1,0:T(8,128)(2,1)S(1)}, bf16[2,256,256]{2,1,0:T(8,128)(2,1)S(1)}, u32[]{:S(2)}, u32[]{:S(2)}) collective-permute-start(bf16[2,256,256]{2,1,0:T(8,128)(2,1)S(1)} %get-tuple-element.40), channel_id=1, source_target_pairs={{0,194},{64,0},{128,64},{192,128},{2,192},{66,2},{130,66},{194,130... | collective-permute-start | bytes 786440 | tf_op jit(solution)/shard_map/ppermute | solution.py:147
  90.5 17.4 %copy-start.12 = (bf16[256,256]{1,0:T(8,128)(2,1)S(1)}, bf16[256,256]{1,0:T(8,128)(2,1)}, u32[]{:S(2)}) copy-start(bf16[256,256]{1,0:T(8,128)(2,1)} %copy-done.11) | copy-start | bytes 393220
  90.6 9.2 %collective-permute-start = (bf16[2,256,256]{2,1,0:T(8,128)(2,1)S(1)}, bf16[2,256,256]{2,1,0:T(8,128)(2,1)S(1)}, u32[]{:S(2)}, u32[]{:S(2)}) collective-permute-start(bf16[2,256,256]{2,1,0:T(8,128)(2,1)S(1)} %get-tuple-element.33), channel_id=1, source_target_pairs={{0,64},{64,128},{128,192},{192,2},{2,66},{66,130},{130,194},{194,0... | collective-permute-start | bytes 786440 | tf_op jit(solution)/shard_map/ppermute | solution.py:147
  90.7 18.8 %copy-start.14 = (bf16[256,256]{1,0:T(8,128)(2,1)S(1)}, bf16[256,256]{1,0:T(8,128)(2,1)}, u32[]{:S(2)}) copy-start(bf16[256,256]{1,0:T(8,128)(2,1)} %copy-done.13) | copy-start | bytes 393220
  90.7 9.2 %collective-permute-start.22 = (bf16[256,256]{1,0:T(8,128)(2,1)S(1)}, bf16[256,256]{1,0:T(8,128)(2,1)S(1)}, u32[]{:S(2)}, u32[]{:S(2)}) collective-permute-start(bf16[256,256]{1,0:T(8,128)(2,1)S(1)} %add_convert_fusion.2), channel_id=1, source_target_pairs={{0,64},{64,128},{128,192},{192,2},{2,66},{66,130},{130,194},{194,0... | collective-permute-start | bytes 393224 | tf_op jit(solution)/shard_map/ppermute | solution.py:147
  90.9 11.5 %collective-permute-start.16 = (bf16[256,256]{1,0:T(8,128)(2,1)S(1)}, bf16[256,256]{1,0:T(8,128)(2,1)S(1)}, u32[]{:S(2)}, u32[]{:S(2)}) collective-permute-start(bf16[256,256]{1,0:T(8,128)(2,1)S(1)} %add_convert_fusion.5), channel_id=1, source_target_pairs={{0,194},{64,0},{128,64},{192,128},{2,192},{66,2},{130,66},{194,130... | collective-permute-start | bytes 393224 | tf_op jit(solution)/shard_map/ppermute | solution.py:147
  93.6 10.1 %collective-permute-start.10 = (bf16[256,256]{1,0:T(8,128)(2,1)S(1)}, bf16[256,256]{1,0:T(8,128)(2,1)S(1)}, u32[]{:S(2)}, u32[]{:S(2)}) collective-permute-start(bf16[256,256]{1,0:T(8,128)(2,1)S(1)} %add_convert_fusion.8), channel_id=1, source_target_pairs={{0,64},{64,128},{128,192},{192,2},{2,66},{66,130},{130,194},{194,0... | collective-permute-start | bytes 393224 | tf_op jit(solution)/shard_map/ppermute | solution.py:147
  96.3 8.7 %collective-permute-start.4 = (bf16[256,256]{1,0:T(8,128)(2,1)S(1)}, bf16[256,256]{1,0:T(8,128)(2,1)S(1)}, u32[]{:S(2)}, u32[]{:S(2)}) collective-permute-start(bf16[256,256]{1,0:T(8,128)(2,1)S(1)} %add_convert_fusion.11), channel_id=1, source_target_pairs={{0,194},{64,0},{128,64},{192,128},{2,192},{66,2},{130,66},{194,130... | collective-permute-start | bytes 393224 | tf_op jit(solution)/shard_map/ppermute | solution.py:147
  99.7 23.9 %copy-start.10 = (bf16[256,256]{1,0:T(8,128)(2,1)S(1)}, bf16[256,256]{1,0:T(8,128)(2,1)}, u32[]{:S(2)}) copy-start(bf16[256,256]{1,0:T(8,128)(2,1)} %copy-done.9) | copy-start | bytes 393220
  99.8 7.5 %collective-permute-start.19 = (bf16[256,256]{1,0:T(8,128)(2,1)S(1)}, bf16[256,256]{1,0:T(8,128)(2,1)S(1)}, u32[]{:S(2)}, u32[]{:S(2)}) collective-permute-start(bf16[256,256]{1,0:T(8,128)(2,1)S(1)} %fusion.2), channel_id=1, source_target_pairs={{0,130},{64,194},{128,0},{192,64},{2,128},{66,192},{130,2},{194,66... | collective-permute-start | bytes 393224 | tf_op jit(solution)/shard_map/ppermute | solution.py:147
  99.9 8.0 %collective-permute-start.13 = (bf16[256,256]{1,0:T(8,128)(2,1)S(1)}, bf16[256,256]{1,0:T(8,128)(2,1)S(1)}, u32[]{:S(2)}, u32[]{:S(2)}) collective-permute-start(bf16[256,256]{1,0:T(8,128)(2,1)S(1)} %fusion.5), channel_id=1, source_target_pairs={{0,128},{64,192},{128,2},{192,66},{2,130},{66,194},{130,0},{194,64... | collective-permute-start | bytes 393224 | tf_op jit(solution)/shard_map/ppermute | solution.py:147
  102.3 21.5 %copy-start.8 = (bf16[256,256]{1,0:T(8,128)(2,1)S(1)}, bf16[256,256]{1,0:T(8,128)(2,1)}, u32[]{:S(2)}) copy-start(bf16[256,256]{1,0:T(8,128)(2,1)} %copy-done.7) | copy-start | bytes 393220
  102.4 9.9 %collective-permute-start.7 = (bf16[256,256]{1,0:T(8,128)(2,1)S(1)}, bf16[256,256]{1,0:T(8,128)(2,1)S(1)}, u32[]{:S(2)}, u32[]{:S(2)}) collective-permute-start(bf16[256,256]{1,0:T(8,128)(2,1)S(1)} %fusion.8), channel_id=1, source_target_pairs={{0,130},{64,194},{128,0},{192,64},{2,128},{66,192},{130,2},{194,66... | collective-permute-start | bytes 393224 | tf_op jit(solution)/shard_map/ppermute | solution.py:147
  103.7 9.7 %collective-permute-start.1 = (bf16[256,256]{1,0:T(8,128)(2,1)S(1)}, bf16[256,256]{1,0:T(8,128)(2,1)S(1)}, u32[]{:S(2)}, u32[]{:S(2)}) collective-permute-start(bf16[256,256]{1,0:T(8,128)(2,1)S(1)} %fusion.11), channel_id=1, source_target_pairs={{0,128},{64,192},{128,2},{192,66},{2,130},{66,194},{130,0},{194,64... | collective-permute-start | bytes 393224 | tf_op jit(solution)/shard_map/ppermute | solution.py:147
  105.0 12.8 %collective-permute-start.23 = (bf16[256,256]{1,0:T(8,128)(2,1)S(1)}, bf16[256,256]{1,0:T(8,128)(2,1)S(1)}, u32[]{:S(2)}, u32[]{:S(2)}) collective-permute-start(bf16[256,256]{1,0:T(8,128)(2,1)S(1)} %add_convert_fusion.1), channel_id=1, source_target_pairs={{0,64},{64,128},{128,192},{192,2},{2,66},{66,130},{130,194},{194,0... | collective-permute-start | bytes 393224 | tf_op jit(solution)/shard_map/ppermute | solution.py:147
  107.2 16.4 %collective-permute-start.17 = (bf16[256,256]{1,0:T(8,128)(2,1)S(1)}, bf16[256,256]{1,0:T(8,128)(2,1)S(1)}, u32[]{:S(2)}, u32[]{:S(2)}) collective-permute-start(bf16[256,256]{1,0:T(8,128)(2,1)S(1)} %add_convert_fusion.4), channel_id=1, source_target_pairs={{0,194},{64,0},{128,64},{192,128},{2,192},{66,2},{130,66},{194,130... | collective-permute-start | bytes 393224 | tf_op jit(solution)/shard_map/ppermute | solution.py:147
  107.9 15.9 %collective-permute-start.11 = (bf16[256,256]{1,0:T(8,128)(2,1)S(1)}, bf16[256,256]{1,0:T(8,128)(2,1)S(1)}, u32[]{:S(2)}, u32[]{:S(2)}) collective-permute-start(bf16[256,256]{1,0:T(8,128)(2,1)S(1)} %add_convert_fusion.7), channel_id=1, source_target_pairs={{0,64},{64,128},{128,192},{192,2},{2,66},{66,130},{130,194},{194,0... | collective-permute-start | bytes 393224 | tf_op jit(solution)/shard_map/ppermute | solution.py:147
  112.2 13.9 %collective-permute-start.5 = (bf16[256,256]{1,0:T(8,128)(2,1)S(1)}, bf16[256,256]{1,0:T(8,128)(2,1)S(1)}, u32[]{:S(2)}, u32[]{:S(2)}) collective-permute-start(bf16[256,256]{1,0:T(8,128)(2,1)S(1)} %add_convert_fusion.10), channel_id=1, source_target_pairs={{0,194},{64,0},{128,64},{192,128},{2,192},{66,2},{130,66},{194,130... | collective-permute-start | bytes 393224 | tf_op jit(solution)/shard_map/ppermute | solution.py:147
  113.4 7.1 %collective-permute-start.20 = (bf16[256,256]{1,0:T(8,128)(2,1)S(1)}, bf16[256,256]{1,0:T(8,128)(2,1)S(1)}, u32[]{:S(2)}, u32[]{:S(2)}) collective-permute-start(bf16[256,256]{1,0:T(8,128)(2,1)S(1)} %fusion.1), channel_id=1, source_target_pairs={{0,194},{64,0},{128,64},{192,128},{2,192},{66,2},{130,66},{194,130... | collective-permute-start | bytes 393224 | tf_op jit(solution)/shard_map/ppermute | solution.py:147
  117.8 6.0 %collective-permute-start.14 = (bf16[256,256]{1,0:T(8,128)(2,1)S(1)}, bf16[256,256]{1,0:T(8,128)(2,1)S(1)}, u32[]{:S(2)}, u32[]{:S(2)}) collective-permute-start(bf16[256,256]{1,0:T(8,128)(2,1)S(1)} %fusion.4), channel_id=1, source_target_pairs={{0,64},{64,128},{128,192},{192,2},{2,66},{66,130},{130,194},{194,0... | collective-permute-start | bytes 393224 | tf_op jit(solution)/shard_map/ppermute | solution.py:147
  120.5 5.5 %collective-permute-start.8 = (bf16[256,256]{1,0:T(8,128)(2,1)S(1)}, bf16[256,256]{1,0:T(8,128)(2,1)S(1)}, u32[]{:S(2)}, u32[]{:S(2)}) collective-permute-start(bf16[256,256]{1,0:T(8,128)(2,1)S(1)} %fusion.7), channel_id=1, source_target_pairs={{0,194},{64,0},{128,64},{192,128},{2,192},{66,2},{130,66},{194,130... | collective-permute-start | bytes 393224 | tf_op jit(solution)/shard_map/ppermute | solution.py:147
  123.7 5.9 %collective-permute-start.2 = (bf16[256,256]{1,0:T(8,128)(2,1)S(1)}, bf16[256,256]{1,0:T(8,128)(2,1)S(1)}, u32[]{:S(2)}, u32[]{:S(2)}) collective-permute-start(bf16[256,256]{1,0:T(8,128)(2,1)S(1)} %fusion.10), channel_id=1, source_target_pairs={{0,64},{64,128},{128,192},{192,2},{2,66},{66,130},{130,194},{194,0... | collective-permute-start | bytes 393224 | tf_op jit(solution)/shard_map/ppermute | solution.py:147
  (9 other events, 14.2 us)
where the time goes:
time: 152 us; the launch traced here: 151 us
  starting transfers between devices  50.8 us (33%)
  waiting for transfers between devices  49.6 us (33%)
  Pallas kernels  22.7 us (15%)
  blocking collectives  20.5 us (13%)
  local copies, waits for them, and re-layouts  5.69 us (4%)
  other arithmetic  1.81 us (1%)
    ppermute x24, starting transfers between devices, shift(): return lax.ppermute(value, COLUMN, ring(step * way))  36.2 us
    all_to_all x2, waiting for transfers between devices, per_device_steps(): got = lax.all_to_all(sent, PLANE, split_axis=0, concat_axis=0, tiled=True)  33.3 us
    all_to_all x1, blocking collectives, per_device_steps(): home = lax.all_to_all(home, PLANE, split_axis=0, concat_axis=0, tiled=True)  20.5 us
    ppermute x24, waiting for transfers between devices, shift(): return lax.ppermute(value, COLUMN, ring(step * way))  16.4 us
    all_to_all x2, starting transfers between devices, per_device_steps(): got = lax.all_to_all(sent, PLANE, split_axis=0, concat_axis=0, tiled=True)  14.6 us
    pallas_call x2, Pallas kernels, per_device_steps(): pl.pallas_call(before, grid=(pairs,), in_specs=[whole((2, 4, 2, 128, 128)...  10.9 us
    pallas_call x4, Pallas kernels, per_device_steps(): pl.pallas_call(functools.partial(after, way), grid=(1,), in_specs=[scalar...  9.21 us
    unnamed x30, local copies, waits for them, and re-layouts  5.69 us
  transfers between devices with their start and end apart: 26, of which 9 were waited for; matrix products, arithmetic and copies ran while one was open for 1% of the time, Pallas kernels for 11%

commit v1 on v0

--- a/solution.py
+++ b/solution.py
@@ -8,7 +8,7 @@
 from jax.sharding import Mesh, PartitionSpec as P
 
 
-SIZES = (2, 2)
+CHUNKS = 2
 PLANE = ("y", "x", "core")
 COLUMN = ("cuts", "zh")
 BF = jnp.bfloat16
@@ -94,22 +94,13 @@
     total = dot(joint_ref[:, :512], jnp.concatenate(states, axis=1))
     total = total + dot(joint_ref[:, 512:], jnp.concatenate(turned, axis=1))
     total = total.astype(BF)
-    first = (4, 2 * way & 7)
-    rest = [place for place in range(8) if place not in first]
-
-    def put(place, value):
-        if place in first:
-            out_refs[0][first.index(place)] = value
-        else:
-            out_refs[1 + rest.index(place)][...] = value
-
     for step in range(4):
         low, high = (total[half * 256 : half * 256 + 256, step * 256 : step * 256 + 256] for half in range(2))
         ahead = (((z + way * step) & 3) - z) & 7
         ahead = jnp.full((256, 256), ahead, jnp.int32)
         place = (way * step) & 3
-        put(place, jnp.where(ahead < 4, low, high))
-        put(place + 4, jnp.where(ahead < 4, high, low))
+        out_refs[place][...] = jnp.where(ahead < 4, low, high)
+        out_refs[place + 4][...] = jnp.where(ahead < 4, high, low)
 
 
 def place(state_ref, out_ref):
@@ -135,23 +126,16 @@
     return total.astype(BF)
 
 
-def reduce_column(arrays, way):
-    pair = arrays[0]
-    rest = [place for place in range(8) if place not in (4, 2 * way & 7)]
-    blocks = {place: array for place, array in zip(rest, arrays[1:])}
-
-    def own(ahead):
-        return blocks[ahead * way & 7]
-
-    def shift(value, step):
-        return lax.ppermute(value, COLUMN, ring(step * way))
-
-    pair, far = shift(pair, 1), shift(own(-3), -1)
-    near, far = add(pair[0], own(3)), add(far, own(-2))
-    near, far = shift(near, 2), shift(far, -1)
-    near, far = add(near, pair[1], own(1)), add(far, own(-1))
-    near, far = shift(near, 1), shift(far, -1)
-    return add(near, far, own(0))
+def reduce_column(blocks, way):
+    near, far = blocks[4], blocks[-3 * way & 7]
+    for step in range(1, 5):
+        near = lax.ppermute(near, COLUMN, ring(way))
+        if step < 4:
+            near = add(near, blocks[(4 - step) * way & 7])
+            far = lax.ppermute(far, COLUMN, ring(-way))
+        if step < 3:
+            far = add(far, blocks[(step - 3) * way & 7])
+    return add(near, far, blocks[0])
 
 
 def shape_of(shape, kind=BF):
@@ -163,6 +147,8 @@
 
 
 def per_device_steps(stem_state, gates):
+    chunks = CHUNKS
+    pairs = 4 // chunks
     z = (lax.axis_index("zh") * 4 + lax.axis_index("cuts")).astype(jnp.int32).reshape(1)
     scalar = pl.BlockSpec(memory_space=pltpu.SMEM)
     local = pl.BlockSpec(memory_space=pltpu.VMEM)
@@ -176,14 +162,13 @@
     )(z, gates)
     state = stem_state.reshape(2, 4, 4, 2, 128, 256)
     sums = []
-    for chunk, pairs in enumerate(SIZES):
-        begin = sum(SIZES[:chunk])
+    for chunk in range(chunks):
         sent = pl.pallas_call(
             before,
             grid=(pairs,),
             in_specs=[
                 whole((2, 4, 2, 128, 128)),
-                pl.BlockSpec((2, 4, 1, 2, 128, 256), lambda hp, begin=begin: (0, 0, begin + hp, 0, 0, 0)),
+                pl.BlockSpec((2, 4, 1, 2, 128, 256), lambda hp, c=chunk: (0, 0, c * pairs + hp, 0, 0, 0)),
             ],
             out_specs=pl.BlockSpec((32, 4, 16, 256), lambda hp: (0, hp, 0, 0)),
             out_shape=shape_of((32, pairs * 4, 16, 256)),
@@ -203,8 +188,8 @@
                 functools.partial(after, way),
                 grid=(1,),
                 in_specs=[scalar, pl.BlockSpec((32, 4, 16, 256), lambda i, pair=pair: (0, pair, 0, 0)), local],
-                out_specs=[local] * 7,
-                out_shape=[pltpu.VMEM((2, 256, 256), BF)] + [pltpu.VMEM((256, 256), BF)] * 6,
+                out_specs=[local] * 8,
+                out_shape=[pltpu.VMEM((256, 256), BF)] * 8,
                 compiler_params=LIMIT,
             )(z, got, joint)
             total = reduce_column(blocks, way)

time: 152 us -> 155 us (1.020)
  blocking collectives: 20.5 us -> 23.4 us
  waiting for transfers between devices: 49.6 us -> 51.7 us
  starting transfers between devices: 50.8 us -> 48.8 us
    all_to_all x1, blocking collectives: 20.5 us -> 23.4 us  [per_device_steps(): home = lax.all_to_all(home, PLANE, split_axis=0, concat_axis=0, tiled=True)]
    ppermute x24 -> x28, waiting for transfers between devices: 16.4 us -> 18.6 us  [the longest x16 16.5 us: reduce_column(): near = lax.ppermute(near, COLUMN, ring(way))]
    ppermute x24 -> x28, starting transfers between devices: 36.2 us -> 34.2 us  [the longest x16 19 us: reduce_column(): near = lax.ppermute(near, COLUMN, ring(way))]
    unnamed x30 -> x38, local copies, waits for them, and re-layouts: 5.69 us -> 5.05 us
  transfers between devices with their start and end apart: 26 -> 30, of which waited for: 9 -> 13; matrix products, arithmetic and copies ran while one was open for 1% -> 2% of each run, Pallas kernels for 11% -> 10%
where the time goes in v1:
time: 155 us; the launch traced here: 154 us
  waiting for transfers between devices  51.7 us (33%)
  starting transfers between devices  48.8 us (31%)
  blocking collectives  23.4 us (15%)
  Pallas kernels  22.1 us (14%)
  local copies, waits for them, and re-layouts  5.05 us (3%)
  other arithmetic  2.82 us (2%)
    all_to_all x2, waiting for transfers between devices, per_device_steps(): got = lax.all_to_all(sent, PLANE, split_axis=0, concat_axis=0, tiled=True)  33.2 us
    all_to_all x1, blocking collectives, per_device_steps(): home = lax.all_to_all(home, PLANE, split_axis=0, concat_axis=0, tiled=True)  23.4 us
    ppermute x16, starting transfers between devices, reduce_column(): near = lax.ppermute(near, COLUMN, ring(way))  19 us
    ppermute x16, waiting for transfers between devices, reduce_column(): near = lax.ppermute(near, COLUMN, ring(way))  16.5 us
    ppermute x12, starting transfers between devices, reduce_column(): far = lax.ppermute(far, COLUMN, ring(-way))  15.2 us
    all_to_all x2, starting transfers between devices, per_device_steps(): got = lax.all_to_all(sent, PLANE, split_axis=0, concat_axis=0, tiled=True)  14.6 us
    pallas_call x2, Pallas kernels, per_device_steps(): pl.pallas_call(before, grid=(pairs,), in_specs=[whole((2, 4, 2, 128, 128)...  10.9 us
    pallas_call x4, Pallas kernels, per_device_steps(): pl.pallas_call(functools.partial(after, way), grid=(1,), in_specs=[scalar...  8.67 us
  transfers between devices with their start and end apart: 30, of which 13 were waited for; matrix products, arithmetic and copies ran while one was open for 2% of the time, Pallas kernels for 10%

profile of v1, /device:TPU:1, one launch (start us, length us, event | category | flops | bytes accessed | tf_op | source)
XLA Modules:
  0.0 154.3 jit_solution(14024834211328585686)
XLA Ops:
  0.0 5.4 %before.3 = bf16[32,8,16,256]{3,2,1,0:T(8,128)(2,1)} custom-call(bf16[2,4,2,128,128]{4,3,2,1,0:T(8,128)(2,1)} %gates_ref.5, bf16[2,4,4,2,128,256]{5,4,3,2,1,0:T(8,128)(2,1)} %bitcast.15), custom_call_target="tpu_custom_call" | custom-call | tf_op jit(solution)/shard_map/before/pallas_call | solution.py:166
  5.4 8.6 %all-to-all-start.1 = ((bf16[32,8,16,256]{3,2,1,0:T(8,128)(2,1)}), bf16[32,8,16,256]{3,2,1,0:T(8,128)(2,1)S(1)}, u32[]{:S(2)}, u32[]{:S(2)}) async-start(bf16[32,8,16,256]{3,2,1,0:T(8,128)(2,1)} %before.3), calls=%async_computation.1 | async-start | bytes 4194304 | tf_op jit(solution)/shard_map/all_to_all | solution.py:182
  14.0 5.5 %before.2 = bf16[32,8,16,256]{3,2,1,0:T(8,128)(2,1)} custom-call(bf16[2,4,2,128,128]{4,3,2,1,0:T(8,128)(2,1)} %gates_ref.5, bf16[2,4,4,2,128,256]{5,4,3,2,1,0:T(8,128)(2,1)} %bitcast.16), custom_call_target="tpu_custom_call" | custom-call | tf_op jit(solution)/shard_map/before/pallas_call | solution.py:166
  19.5 23.1 %all-to-all-done.1.state_ref = bf16[32,8,16,256]{3,2,1,0:T(8,128)(2,1)S(1)} async-done(((bf16[32,8,16,256]{3,2,1,0:T(8,128)(2,1)}), bf16[32,8,16,256]{3,2,1,0:T(8,128)(2,1)S(1)}, u32[]{:S(2)}, u32[]{:S(2)}) %all-to-all-start.1) | async-done | bytes 2097184 | tf_op jit(solution)/shard_map/all_to_all | solution.py:182
  42.6 6.1 %all-to-all-start = ((bf16[32,8,16,256]{3,2,1,0:T(8,128)(2,1)}), bf16[32,8,16,256]{3,2,1,0:T(8,128)(2,1)}, u32[]{:S(2)}, u32[]{:S(2)}) async-start(bf16[32,8,16,256]{3,2,1,0:T(8,128)(2,1)} %before.2), calls=%async_computation | async-start | bytes 4194304 | tf_op jit(solution)/shard_map/all_to_all | solution.py:182
  51.0 1.8 %shard_map.31 = (bf16[256,256]{1,0:T(8,128)(2,1)S(1)}, bf16[256,256]{1,0:T(8,128)(2,1)S(1)}, bf16[256,256]{1,0:T(8,128)(2,1)S(1)}, bf16[256,256]{1,0:T(8,128)(2,...) custom-call(s32[1]{0:T(128)} %bitcast.z_ref, ...), custom_call_target="tpu_custom_call" | custom-call | tf_op jit(solution)/shard_map/pallas_call | solution.py:187
  54.2 5.6 %collective-permute-start.21 = (bf16[256,256]{1,0:T(8,128)(2,1)}, bf16[256,256]{1,0:T(8,128)(2,1)}, u32[]{:S(2)}, u32[]{:S(2)}) collective-permute-start(bf16[256,256]{1,0:T(8,128)(2,1)} %get-tuple-element.61), channel_id=1, source_target_pairs={{0,194},{64,0},{128,64},{192,128},{2,192},{66,2},{130,66},{194,130... | collective-permute-start | bytes 393224 | tf_op jit(solution)/shard_map/ppermute | solution.py:132
  59.8 1.9 %shard_map.30 = (bf16[256,256]{1,0:T(8,128)(2,1)S(1)}, bf16[256,256]{1,0:T(8,128)(2,1)S(1)}, bf16[256,256]{1,0:T(8,128)(2,1)S(1)}, bf16[256,256]{1,0:T(8,128)(2,...) custom-call(s32[1]{0:T(128)} %bitcast.z_ref, ...), custom_call_target="tpu_custom_call" | custom-call | tf_op jit(solution)/shard_map/pallas_call | solution.py:187
  64.3 2.7 %collective-permute-start.18 = (bf16[256,256]{1,0:T(8,128)(2,1)}, bf16[256,256]{1,0:T(8,128)(2,1)S(1)}, u32[]{:S(2)}, u32[]{:S(2)}) collective-permute-start(bf16[256,256]{1,0:T(8,128)(2,1)} %get-tuple-element.57), channel_id=1, source_target_pairs={{0,194},{64,0},{128,64},{192,128},{2,192},{66,2},{130,66},{194,130... | collective-permute-start | bytes 393224 | tf_op jit(solution)/shard_map/ppermute | solution.py:135
  67.0 10.0 %all-to-all-done.state_ref = bf16[32,8,16,256]{3,2,1,0:T(8,128)(2,1)} async-done(((bf16[32,8,16,256]{3,2,1,0:T(8,128)(2,1)}), bf16[32,8,16,256]{3,2,1,0:T(8,128)(2,1)}, u32[]{:S(2)}, u32[]{:S(2)}) %all-to-all-start) | async-done | bytes 2097184 | tf_op jit(solution)/shard_map/all_to_all | solution.py:182
  77.0 2.5 %shard_map.29 = (bf16[256,256]{1,0:T(8,128)(2,1)S(1)}, bf16[256,256]{1,0:T(8,128)(2,1)S(1)}, bf16[256,256]{1,0:T(8,128)(2,1)S(1)}, bf16[256,256]{1,0:T(8,128)(2,...) custom-call(s32[1]{0:T(128)} %bitcast.z_ref, ...), custom_call_target="tpu_custom_call" | custom-call | tf_op jit(solution)/shard_map/pallas_call | solution.py:187
  79.6 5.8 %collective-permute-start.7 = (bf16[256,256]{1,0:T(8,128)(2,1)S(1)}, bf16[256,256]{1,0:T(8,128)(2,1)S(1)}, u32[]{:S(2)}, u32[]{:S(2)}) collective-permute-start(bf16[256,256]{1,0:T(8,128)(2,1)S(1)} %get-tuple-element.45), channel_id=1, source_target_pairs={{0,194},{64,0},{128,64},{192,128},{2,192},{66,2},{130,66},{194,130... | collective-permute-start | bytes 393224 | tf_op jit(solution)/shard_map/ppermute | solution.py:132
  85.4 2.5 %shard_map.28 = (bf16[256,256]{1,0:T(8,128)(2,1)S(1)}, bf16[256,256]{1,0:T(8,128)(2,1)S(1)}, bf16[256,256]{1,0:T(8,128)(2,1)S(1)}, bf16[256,256]{1,0:T(8,128)(2,...) custom-call(s32[1]{0:T(128)} %bitcast.z_ref, ...), custom_call_target="tpu_custom_call" | custom-call | tf_op jit(solution)/shard_map/pallas_call | solution.py:187
  90.1 2.7 %collective-permute-start.4 = (bf16[256,256]{1,0:T(8,128)(2,1)S(1)}, bf16[256,256]{1,0:T(8,128)(2,1)S(1)}, u32[]{:S(2)}, u32[]{:S(2)}) collective-permute-start(bf16[256,256]{1,0:T(8,128)(2,1)S(1)} %get-tuple-element.41), channel_id=1, source_target_pairs={{0,194},{64,0},{128,64},{192,128},{2,192},{66,2},{130,66},{194,130... | collective-permute-start | bytes 393224 | tf_op jit(solution)/shard_map/ppermute | solution.py:135
  92.9 1.5 collective-permute-start.22
  94.8 2.7 %collective-permute-start.19 = (bf16[256,256]{1,0:T(8,128)(2,1)S(1)}, bf16[256,256]{1,0:T(8,128)(2,1)S(1)}, u32[]{:S(2)}, u32[]{:S(2)}) collective-permute-start(bf16[256,256]{1,0:T(8,128)(2,1)S(1)} %add_convert_fusion.8), channel_id=1, source_target_pairs={{0,194},{64,0},{128,64},{192,128},{2,192},{66,2},{130,66},{194,130... | collective-permute-start | bytes 393224 | tf_op jit(solution)/shard_map/ppermute | solution.py:135
  97.5 1.5 collective-permute-start.8
  99.6 1.4 collective-permute-done.15
  100.9 1.4 collective-permute-start.5
  102.4 1.3 collective-permute-start.23
  104.1 1.8 %collective-permute-done.12 = bf16[256,256]{1,0:T(8,128)(2,1)S(1)} collective-permute-done((bf16[256,256]{1,0:T(8,128)(2,1)S(1)}, bf16[256,256]{1,0:T(8,128)(2,1)S(1)}, u32[]{:S(2)}, u32[]{:S(2)}) %collective-permute-start.12) | collective-permute-done | bytes 131104 | tf_op jit(solution)/shard_map/ppermute | solution.py:135
  105.9 1.8 %collective-permute-done.1 = bf16[256,256]{1,0:T(8,128)(2,1)S(1)} collective-permute-done((bf16[256,256]{1,0:T(8,128)(2,1)S(1)}, bf16[256,256]{1,0:T(8,128)(2,1)S(1)}, u32[]{:S(2)}, u32[]{:S(2)}) %collective-permute-start.1) | collective-permute-done | bytes 131104 | tf_op jit(solution)/shard_map/ppermute | solution.py:132
  109.1 1.5 collective-permute-start.13
  110.6 2.9 %collective-permute-done.16 = bf16[256,256]{1,0:T(8,128)(2,1)S(1)} collective-permute-done((bf16[256,256]{1,0:T(8,128)(2,1)S(1)}, bf16[256,256]{1,0:T(8,128)(2,1)S(1)}, u32[]{:S(2)}, u32[]{:S(2)}) %collective-permute-start.16) | collective-permute-done | bytes 131104 | tf_op jit(solution)/shard_map/ppermute | solution.py:132
  113.5 2.0 %collective-permute-done.9 = bf16[256,256]{1,0:T(8,128)(2,1)S(1)} collective-permute-done((bf16[256,256]{1,0:T(8,128)(2,1)S(1)}, bf16[256,256]{1,0:T(8,128)(2,1)S(1)}, u32[]{:S(2)}, u32[]{:S(2)}) %collective-permute-start.9) | collective-permute-done | bytes 131104 | tf_op jit(solution)/shard_map/ppermute | solution.py:132
  115.6 2.2 %collective-permute-start.6 = (bf16[256,256]{1,0:T(8,128)(2,1)S(1)}, bf16[256,256]{1,0:T(8,128)(2,1)S(1)}, u32[]{:S(2)}, u32[]{:S(2)}) collective-permute-start(bf16[256,256]{1,0:T(8,128)(2,1)S(1)} %add_convert_fusion.19), channel_id=1, source_target_pairs={{0,194},{64,0},{128,64},{192,128},{2,192},{66,2},{130,66},{194,130... | collective-permute-start | bytes 393224 | tf_op jit(solution)/shard_map/ppermute | solution.py:135
  119.0 1.5 collective-permute-start.17
  120.6 2.5 %collective-permute-done.24 = bf16[256,256]{1,0:T(8,128)(2,1)S(1)} collective-permute-done((bf16[256,256]{1,0:T(8,128)(2,1)S(1)}, bf16[256,256]{1,0:T(8,128)(2,1)S(1)}, u32[]{:S(2)}, u32[]{:S(2)}) %collective-permute-start.24) | collective-permute-done | bytes 131104 | tf_op jit(solution)/shard_map/ppermute | solution.py:132
  123.1 1.3 collective-permute-start.10
  125.9 1.8 %collective-permute-done.10 = bf16[256,256]{1,0:T(8,128)(2,1)S(1)} collective-permute-done((bf16[256,256]{1,0:T(8,128)(2,1)S(1)}, bf16[256,256]{1,0:T(8,128)(2,1)S(1)}, u32[]{:S(2)}, u32[]{:S(2)}) %collective-permute-start.10) | collective-permute-done | bytes 131104 | tf_op jit(solution)/shard_map/ppermute | solution.py:132
  127.7 1.8 %collective-permute-done.3 = bf16[256,256]{1,0:T(8,128)(2,1)S(1)} collective-permute-done((bf16[256,256]{1,0:T(8,128)(2,1)S(1)}, bf16[256,256]{1,0:T(8,128)(2,1)S(1)}, u32[]{:S(2)}, u32[]{:S(2)}) %collective-permute-start.3) | collective-permute-done | bytes 131104 | tf_op jit(solution)/shard_map/ppermute | solution.py:132
  129.7 23.4 %all_to_all.15.state_ref = bf16[32,4,8,256]{3,2,1,0:T(8,128)(2,1)S(1)} all-to-all(bf16[32,4,8,256]{3,2,1,0:T(8,128)(2,1)S(1)} %maximum_bitcast_fusion), channel_id=1, replica_groups=mesh['cuts'=4,'y'=4,'x'=4,'zh'=2,'core'=2] {'y','x','core'}, dimensions={0} | all-to-all | bytes 1048576 | tf_op jit(solution)/shard_map/all_to_all | solution.py:198
  (100 shorter events, 15.4 us)
Async XLA Ops:
  5.4 37.2 %all-to-all-start.1 = ((bf16[32,8,16,256]{3,2,1,0:T(8,128)(2,1)}), bf16[32,8,16,256]{3,2,1,0:T(8,128)(2,1)S(1)}, u32[]{:S(2)}, u32[]{:S(2)}) async-start(bf16[32,8,16,256]{3,2,1,0:T(8,128)(2,1)} %before.3), calls=%async_computation.1 | async-start | bytes 4194304 | tf_op jit(solution)/shard_map/all_to_all | solution.py:182
  42.6 34.4 %all-to-all-start = ((bf16[32,8,16,256]{3,2,1,0:T(8,128)(2,1)}), bf16[32,8,16,256]{3,2,1,0:T(8,128)(2,1)}, u32[]{:S(2)}, u32[]{:S(2)}) async-start(bf16[32,8,16,256]{3,2,1,0:T(8,128)(2,1)} %before.2), calls=%async_computation | async-start | bytes 4194304 | tf_op jit(solution)/shard_map/all_to_all | solution.py:182
  54.2 33.8 %collective-permute-start.21 = (bf16[256,256]{1,0:T(8,128)(2,1)}, bf16[256,256]{1,0:T(8,128)(2,1)}, u32[]{:S(2)}, u32[]{:S(2)}) collective-permute-start(bf16[256,256]{1,0:T(8,128)(2,1)} %get-tuple-element.61), channel_id=1, source_target_pairs={{0,194},{64,0},{128,64},{192,128},{2,192},{66,2},{130,66},{194,130... | collective-permute-start | bytes 393224 | tf_op jit(solution)/shard_map/ppermute | solution.py:132
  59.7 29.3 %collective-permute-start.25 = (bf16[256,256]{1,0:T(8,128)(2,1)}, bf16[256,256]{1,0:T(8,128)(2,1)}, u32[]{:S(2)}, u32[]{:S(2)}) collective-permute-start(bf16[256,256]{1,0:T(8,128)(2,1)} %get-tuple-element.65), channel_id=1, source_target_pairs={{0,64},{64,128},{128,192},{192,2},{2,66},{66,130},{130,194},{194,0... | collective-permute-start | bytes 393224 | tf_op jit(solution)/shard_map/ppermute | solution.py:135
  64.2 25.9 %collective-permute-start.14 = (bf16[256,256]{1,0:T(8,128)(2,1)}, bf16[256,256]{1,0:T(8,128)(2,1)S(1)}, u32[]{:S(2)}, u32[]{:S(2)}) collective-permute-start(bf16[256,256]{1,0:T(8,128)(2,1)} %get-tuple-element.53), channel_id=1, source_target_pairs={{0,64},{64,128},{128,192},{192,2},{2,66},{66,130},{130,194},{194,0... | collective-permute-start | bytes 393224 | tf_op jit(solution)/shard_map/ppermute | solution.py:132
  64.3 28.6 %collective-permute-start.18 = (bf16[256,256]{1,0:T(8,128)(2,1)}, bf16[256,256]{1,0:T(8,128)(2,1)S(1)}, u32[]{:S(2)}, u32[]{:S(2)}) collective-permute-start(bf16[256,256]{1,0:T(8,128)(2,1)} %get-tuple-element.57), channel_id=1, source_target_pairs={{0,194},{64,0},{128,64},{192,128},{2,192},{66,2},{130,66},{194,130... | collective-permute-start | bytes 393224 | tf_op jit(solution)/shard_map/ppermute | solution.py:135
  79.6 14.8 %collective-permute-start.7 = (bf16[256,256]{1,0:T(8,128)(2,1)S(1)}, bf16[256,256]{1,0:T(8,128)(2,1)S(1)}, u32[]{:S(2)}, u32[]{:S(2)}) collective-permute-start(bf16[256,256]{1,0:T(8,128)(2,1)S(1)} %get-tuple-element.45), channel_id=1, source_target_pairs={{0,194},{64,0},{128,64},{192,128},{2,192},{66,2},{130,66},{194,130... | collective-permute-start | bytes 393224 | tf_op jit(solution)/shard_map/ppermute | solution.py:132
  88.0 6.6 %collective-permute-start.11 = (bf16[256,256]{1,0:T(8,128)(2,1)S(1)}, bf16[256,256]{1,0:T(8,128)(2,1)S(1)}, u32[]{:S(2)}, u32[]{:S(2)}) collective-permute-start(bf16[256,256]{1,0:T(8,128)(2,1)S(1)} %get-tuple-element.49), channel_id=1, source_target_pairs={{0,64},{64,128},{128,192},{192,2},{2,66},{66,130},{130,194},{194,0... | collective-permute-start | bytes 393224 | tf_op jit(solution)/shard_map/ppermute | solution.py:135
  89.1 5.7 %collective-permute-start = (bf16[256,256]{1,0:T(8,128)(2,1)S(1)}, bf16[256,256]{1,0:T(8,128)(2,1)S(1)}, u32[]{:S(2)}, u32[]{:S(2)}) collective-permute-start(bf16[256,256]{1,0:T(8,128)(2,1)S(1)} %get-tuple-element.37), channel_id=1, source_target_pairs={{0,64},{64,128},{128,192},{192,2},{2,66},{66,130},{130,194},{194,0... | collective-permute-start | bytes 393224 | tf_op jit(solution)/shard_map/ppermute | solution.py:132
  90.1 7.4 %collective-permute-start.4 = (bf16[256,256]{1,0:T(8,128)(2,1)S(1)}, bf16[256,256]{1,0:T(8,128)(2,1)S(1)}, u32[]{:S(2)}, u32[]{:S(2)}) collective-permute-start(bf16[256,256]{1,0:T(8,128)(2,1)S(1)} %get-tuple-element.41), channel_id=1, source_target_pairs={{0,194},{64,0},{128,64},{192,128},{2,192},{66,2},{130,66},{194,130... | collective-permute-start | bytes 393224 | tf_op jit(solution)/shard_map/ppermute | solution.py:135
  92.9 6.2 %collective-permute-start.22 = (bf16[256,256]{1,0:T(8,128)(2,1)S(1)}, bf16[256,256]{1,0:T(8,128)(2,1)S(1)}, u32[]{:S(2)}, u32[]{:S(2)}) collective-permute-start(bf16[256,256]{1,0:T(8,128)(2,1)S(1)} %add_convert_fusion.5), channel_id=1, source_target_pairs={{0,194},{64,0},{128,64},{192,128},{2,192},{66,2},{130,66},{194,130... | collective-permute-start | bytes 393224 | tf_op jit(solution)/shard_map/ppermute | solution.py:132
  94.4 5.1 %collective-permute-start.26 = (bf16[256,256]{1,0:T(8,128)(2,1)S(1)}, bf16[256,256]{1,0:T(8,128)(2,1)S(1)}, u32[]{:S(2)}, u32[]{:S(2)}) collective-permute-start(bf16[256,256]{1,0:T(8,128)(2,1)S(1)} %add_convert_fusion.2), channel_id=1, source_target_pairs={{0,64},{64,128},{128,192},{192,2},{2,66},{66,130},{130,194},{194,0... | collective-permute-start | bytes 393224 | tf_op jit(solution)/shard_map/ppermute | solution.py:135
  94.6 6.3 %collective-permute-start.15 = (bf16[256,256]{1,0:T(8,128)(2,1)S(1)}, bf16[256,256]{1,0:T(8,128)(2,1)S(1)}, u32[]{:S(2)}, u32[]{:S(2)}) collective-permute-start(bf16[256,256]{1,0:T(8,128)(2,1)S(1)} %add_convert_fusion.11), channel_id=1, source_target_pairs={{0,64},{64,128},{128,192},{192,2},{2,66},{66,130},{130,194},{194,0... | collective-permute-start | bytes 393224 | tf_op jit(solution)/shard_map/ppermute | solution.py:132
  94.8 7.6 %collective-permute-start.19 = (bf16[256,256]{1,0:T(8,128)(2,1)S(1)}, bf16[256,256]{1,0:T(8,128)(2,1)S(1)}, u32[]{:S(2)}, u32[]{:S(2)}) collective-permute-start(bf16[256,256]{1,0:T(8,128)(2,1)S(1)} %add_convert_fusion.8), channel_id=1, source_target_pairs={{0,194},{64,0},{128,64},{192,128},{2,192},{66,2},{130,66},{194,130... | collective-permute-start | bytes 393224 | tf_op jit(solution)/shard_map/ppermute | solution.py:135
  97.5 6.2 %collective-permute-start.8 = (bf16[256,256]{1,0:T(8,128)(2,1)S(1)}, bf16[256,256]{1,0:T(8,128)(2,1)S(1)}, u32[]{:S(2)}, u32[]{:S(2)}) collective-permute-start(bf16[256,256]{1,0:T(8,128)(2,1)S(1)} %add_convert_fusion.17), channel_id=1, source_target_pairs={{0,194},{64,0},{128,64},{192,128},{2,192},{66,2},{130,66},{194,130... | collective-permute-start | bytes 393224 | tf_op jit(solution)/shard_map/ppermute | solution.py:132
  99.1 6.8 %collective-permute-start.12 = (bf16[256,256]{1,0:T(8,128)(2,1)S(1)}, bf16[256,256]{1,0:T(8,128)(2,1)S(1)}, u32[]{:S(2)}, u32[]{:S(2)}) collective-permute-start(bf16[256,256]{1,0:T(8,128)(2,1)S(1)} %add_convert_fusion.14), channel_id=1, source_target_pairs={{0,64},{64,128},{128,192},{192,2},{2,66},{66,130},{130,194},{194,0... | collective-permute-start | bytes 393224 | tf_op jit(solution)/shard_map/ppermute | solution.py:135
  99.5 8.2 %collective-permute-start.1 = (bf16[256,256]{1,0:T(8,128)(2,1)S(1)}, bf16[256,256]{1,0:T(8,128)(2,1)S(1)}, u32[]{:S(2)}, u32[]{:S(2)}) collective-permute-start(bf16[256,256]{1,0:T(8,128)(2,1)S(1)} %add_convert_fusion.23), channel_id=1, source_target_pairs={{0,64},{64,128},{128,192},{192,2},{2,66},{66,130},{130,194},{194,0... | collective-permute-start | bytes 393224 | tf_op jit(solution)/shard_map/ppermute | solution.py:132
  99.5 24.8 %copy-start.16 = (bf16[256,256]{1,0:T(8,128)(2,1)S(1)}, bf16[256,256]{1,0:T(8,128)(2,1)}, u32[]{:S(2)}) copy-start(bf16[256,256]{1,0:T(8,128)(2,1)} %copy-done.15) | copy-start | bytes 393220
  100.9 8.0 %collective-permute-start.5 = (bf16[256,256]{1,0:T(8,128)(2,1)S(1)}, bf16[256,256]{1,0:T(8,128)(2,1)S(1)}, u32[]{:S(2)}, u32[]{:S(2)}) collective-permute-start(bf16[256,256]{1,0:T(8,128)(2,1)S(1)} %add_convert_fusion.20), channel_id=1, source_target_pairs={{0,194},{64,0},{128,64},{192,128},{2,192},{66,2},{130,66},{194,130... | collective-permute-start | bytes 393224 | tf_op jit(solution)/shard_map/ppermute | solution.py:135
  102.4 23.4 %copy-start.18 = (bf16[256,256]{1,0:T(8,128)(2,1)S(1)}, bf16[256,256]{1,0:T(8,128)(2,1)}, u32[]{:S(2)}) copy-start(bf16[256,256]{1,0:T(8,128)(2,1)} %copy-done.17) | copy-start | bytes 393220
  102.4 6.7 %collective-permute-start.23 = (bf16[256,256]{1,0:T(8,128)(2,1)S(1)}, bf16[256,256]{1,0:T(8,128)(2,1)S(1)}, u32[]{:S(2)}, u32[]{:S(2)}) collective-permute-start(bf16[256,256]{1,0:T(8,128)(2,1)S(1)} %add_convert_fusion.4), channel_id=1, source_target_pairs={{0,194},{64,0},{128,64},{192,128},{2,192},{66,2},{130,66},{194,130... | collective-permute-start | bytes 393224 | tf_op jit(solution)/shard_map/ppermute | solution.py:132
  103.7 15.3 %collective-permute-start.27 = (bf16[256,256]{1,0:T(8,128)(2,1)S(1)}, bf16[256,256]{1,0:T(8,128)(2,1)S(1)}, u32[]{:S(2)}, u32[]{:S(2)}) collective-permute-start(bf16[256,256]{1,0:T(8,128)(2,1)S(1)} %add_convert_fusion.1), channel_id=1, source_target_pairs={{0,64},{64,128},{128,192},{192,2},{2,66},{66,130},{130,194},{194,0... | collective-permute-start | bytes 393224 | tf_op jit(solution)/shard_map/ppermute | solution.py:135
  105.9 7.6 %collective-permute-start.16 = (bf16[256,256]{1,0:T(8,128)(2,1)S(1)}, bf16[256,256]{1,0:T(8,128)(2,1)S(1)}, u32[]{:S(2)}, u32[]{:S(2)}) collective-permute-start(bf16[256,256]{1,0:T(8,128)(2,1)S(1)} %add_convert_fusion.10), channel_id=1, source_target_pairs={{0,64},{64,128},{128,192},{192,2},{2,66},{66,130},{130,194},{194,0... | collective-permute-start | bytes 393224 | tf_op jit(solution)/shard_map/ppermute | solution.py:132
  107.7 16.7 %collective-permute-start.20 = (bf16[256,256]{1,0:T(8,128)(2,1)S(1)}, bf16[256,256]{1,0:T(8,128)(2,1)S(1)}, u32[]{:S(2)}, u32[]{:S(2)}) collective-permute-start(bf16[256,256]{1,0:T(8,128)(2,1)S(1)} %add_convert_fusion.7), channel_id=1, source_target_pairs={{0,194},{64,0},{128,64},{192,128},{2,192},{66,2},{130,66},{194,130... | collective-permute-start | bytes 393224 | tf_op jit(solution)/shard_map/ppermute | solution.py:135
  108.9 6.6 %collective-permute-start.9 = (bf16[256,256]{1,0:T(8,128)(2,1)S(1)}, bf16[256,256]{1,0:T(8,128)(2,1)S(1)}, u32[]{:S(2)}, u32[]{:S(2)}) collective-permute-start(bf16[256,256]{1,0:T(8,128)(2,1)S(1)} %add_convert_fusion.16), channel_id=1, source_target_pairs={{0,194},{64,0},{128,64},{192,128},{2,192},{66,2},{130,66},{194,130... | collective-permute-start | bytes 393224 | tf_op jit(solution)/shard_map/ppermute | solution.py:132
  109.1 16.7 %collective-permute-start.13 = (bf16[256,256]{1,0:T(8,128)(2,1)S(1)}, bf16[256,256]{1,0:T(8,128)(2,1)S(1)}, u32[]{:S(2)}, u32[]{:S(2)}) collective-permute-start(bf16[256,256]{1,0:T(8,128)(2,1)S(1)} %add_convert_fusion.13), channel_id=1, source_target_pairs={{0,64},{64,128},{128,192},{192,2},{2,66},{66,130},{130,194},{194,0... | collective-permute-start | bytes 393224 | tf_op jit(solution)/shard_map/ppermute | solution.py:135
  113.5 5.5 %collective-permute-start.2 = (bf16[256,256]{1,0:T(8,128)(2,1)S(1)}, bf16[256,256]{1,0:T(8,128)(2,1)S(1)}, u32[]{:S(2)}, u32[]{:S(2)}) collective-permute-start(bf16[256,256]{1,0:T(8,128)(2,1)S(1)} %add_convert_fusion.22), channel_id=1, source_target_pairs={{0,64},{64,128},{128,192},{192,2},{2,66},{66,130},{130,194},{194,0... | collective-permute-start | bytes 393224 | tf_op jit(solution)/shard_map/ppermute | solution.py:132
  115.6 12.1 %collective-permute-start.6 = (bf16[256,256]{1,0:T(8,128)(2,1)S(1)}, bf16[256,256]{1,0:T(8,128)(2,1)S(1)}, u32[]{:S(2)}, u32[]{:S(2)}) collective-permute-start(bf16[256,256]{1,0:T(8,128)(2,1)S(1)} %add_convert_fusion.19), channel_id=1, source_target_pairs={{0,194},{64,0},{128,64},{192,128},{2,192},{66,2},{130,66},{194,130... | collective-permute-start | bytes 393224 | tf_op jit(solution)/shard_map/ppermute | solution.py:135
  119.0 4.1 %collective-permute-start.24 = (bf16[256,256]{1,0:T(8,128)(2,1)S(1)}, bf16[256,256]{1,0:T(8,128)(2,1)S(1)}, u32[]{:S(2)}, u32[]{:S(2)}) collective-permute-start(bf16[256,256]{1,0:T(8,128)(2,1)S(1)} %add_convert_fusion.3), channel_id=1, source_target_pairs={{0,194},{64,0},{128,64},{192,128},{2,192},{66,2},{130,66},{194,130... | collective-permute-start | bytes 393224 | tf_op jit(solution)/shard_map/ppermute | solution.py:132
  119.0 6.8 %collective-permute-start.17 = (bf16[256,256]{1,0:T(8,128)(2,1)S(1)}, bf16[256,256]{1,0:T(8,128)(2,1)S(1)}, u32[]{:S(2)}, u32[]{:S(2)}) collective-permute-start(bf16[256,256]{1,0:T(8,128)(2,1)S(1)} %add_convert_fusion.9), channel_id=1, source_target_pairs={{0,64},{64,128},{128,192},{192,2},{2,66},{66,130},{130,194},{194,0... | collective-permute-start | bytes 393224 | tf_op jit(solution)/shard_map/ppermute | solution.py:132
  123.1 4.6 %collective-permute-start.10 = (bf16[256,256]{1,0:T(8,128)(2,1)S(1)}, bf16[256,256]{1,0:T(8,128)(2,1)S(1)}, u32[]{:S(2)}, u32[]{:S(2)}) collective-permute-start(bf16[256,256]{1,0:T(8,128)(2,1)S(1)} %add_convert_fusion.15), channel_id=1, source_target_pairs={{0,194},{64,0},{128,64},{192,128},{2,192},{66,2},{130,66},{194,130... | collective-permute-start | bytes 393224 | tf_op jit(solution)/shard_map/ppermute | solution.py:132
  124.4 5.1 %collective-permute-start.3 = (bf16[256,256]{1,0:T(8,128)(2,1)S(1)}, bf16[256,256]{1,0:T(8,128)(2,1)S(1)}, u32[]{:S(2)}, u32[]{:S(2)}) collective-permute-start(bf16[256,256]{1,0:T(8,128)(2,1)S(1)} %add_convert_fusion.21), channel_id=1, source_target_pairs={{0,64},{64,128},{128,192},{192,2},{2,66},{66,130},{130,194},{194,0... | collective-permute-start | bytes 393224 | tf_op jit(solution)/shard_map/ppermute | solution.py:132
  (17 other events, 116.0 us)
